TPU v7x, 32 devices: a whole 2x2x4 slice. The times are simulated.
32 devices in a mesh: segment: 4 (over y, core), row: 8 (over z, x).
Axes of the slice: x: 2, y: 2, z: 4, core: 2. Of those that a mesh axis runs over, the one named last changes fastest.
Arguments:
- snapshots: float32 [2048, 512], P('row', 'segment'), may hold values from -6 to 6
- basis: float32 [2048, 2048], P('row', 'segment'), may hold values from -0.125 to 0.125
Outputs:
- residual: float32 [2048, 512], P('row', 'segment')
- coefficients: float32 [2048, 512], P('segment')
- residual_rms: float32 [512], P('segment')
All inputs are finite; a program needn't handle non-finite values.
Results may differ from a plain program's by a relative error of at most 0.0001.
Values sent between devices are 32-bit elements; how exact they have to be, the bound alone decides.
A program may use at most 64 MiB of HBM per device.

v0:
```python
import jax
import jax.numpy as jnp
from jax import lax
from jax.sharding import PartitionSpec as P

TICKS = 2


def shifted(value, axis, steps):
    count = lax.axis_size(axis)
    pairs = [(source, (source + steps) % count) for source in range(count)]
    return lax.ppermute(value, axis, pairs)


def per_device(snapshots, basis):
    high = lax.Precision.HIGHEST
    sections = lax.axis_size("segment")
    position = lax.axis_index("segment")
    width = snapshots.shape[1]
    total_rows = basis.shape[0] * lax.axis_size("row")
    gram = lax.psum(
        jnp.dot(basis.T, basis, precision=high, preferred_element_type=jnp.float32), "row"
    )
    coeff = jnp.zeros((basis.shape[1], width * sections), jnp.float32)
    vec = snapshots
    for step in range(TICKS):
        visit_vec = vec
        visit_coeff = coeff
        owner = (position - step) % sections
        first = lax.psum(
            jnp.dot(basis.T, visit_vec, precision=high, preferred_element_type=jnp.float32), "row"
        )
        moved = visit_vec - jnp.dot(
            basis, first, precision=high, preferred_element_type=jnp.float32
        )
        second = first - jnp.dot(gram, first, precision=high, preferred_element_type=jnp.float32)
        visit_vec = moved - jnp.dot(
            basis, second, precision=high, preferred_element_type=jnp.float32
        )
        visit_coeff = lax.dynamic_update_slice(
            visit_coeff, first + second, (jnp.int32(0), owner * width)
        )
        vec = visit_vec
        coeff = visit_coeff
        if step + 1 < TICKS:
            vec = shifted(vec, "segment", 1)
    vec = shifted(vec, "segment", 1 - TICKS)
    sums = lax.psum(jnp.sum(vec * vec, axis=0), "row")
    rms = jnp.sqrt(sums / total_rows)
    return (vec, coeff, rms)


def solution(mesh):
    placed = (P("row", "segment"), P("row", "segment"))
    return jax.shard_map(
        per_device,
        mesh=mesh,
        in_specs=placed,
        out_specs=(P("row", "segment"), P("segment", None), P("segment")),
        check_vma=False,
    )
```

profile of v0, /device:TPU:0, one launch (start us, length us, event | category | flops | bytes accessed | tf_op | source)
XLA Modules:
  0.0 212.9 jit_solution(10903807755244072414)
XLA Ops:
  7.2 1.0 copy-done
  8.2 2.0 fusion.6
  10.2 1.7 fusion.5
  12.0 0.1 copy.5
  12.1 86.5 %all-reduce.6.cloned.1.call-done = (f32[512,128]{1,0:T(8,128)}, f32[512,512]{1,0:T(8,128)}) async-done(((f32[512,128]{1,0:T(8,128)}, f32[512,512]{1,0:T(8,128)}), (f32[512,128]{1,0:T(8,128)}, f32[512,512]{1,0:T(8,128)})) %all-reduce.6.cloned.1.call-update) | async-done | bytes 1310736 | tf_op jit(solution)/shard_map/psum | solution.py:30
  98.7 1.6 fusion.3
  100.3 0.1 broadcast_in_dim.3
  100.5 0.8 copy-done.4
  101.3 1.0 add_dynamic-update-slice_fusion
  102.3 0.6 fusion.2
  102.9 0.1 collective-permute-start
  102.9 4.4 %collective-permute-done = f32[256,128]{0,1:T(8,128)S(1)} collective-permute-done((f32[256,128]{0,1:T(8,128)S(1)}, f32[256,128]{0,1:T(8,128)S(1)}, u32[]{:S(2)}, u32[]{:S(2)}) %collective-permute-start) | collective-permute-done | bytes 131104 | tf_op jit(solution)/shard_map/ppermute | solution.py:12
  107.3 1.1 convolution_bitcast_fusion
  108.4 70.2 %all-reduce.4.cloned.1.call-done = f32[512,128]{0,1:T(8,128)} async-done(((f32[512,128]{0,1:T(8,128)}), f32[512,128]{0,1:T(8,128)}) %all-reduce.4.cloned.1.call-update) | async-done | bytes 262160 | tf_op jit(solution)/shard_map/psum | solution.py:30
  178.7 2.2 %fusion.4 = (f32[512,128]{0,1:T(8,128)S(1)}, f32[512,128]{0,1:T(8,128)S(1)}) fusion(f32[512,128]{0,1:T(8,128)} %all-reduce.4.cloned.1.call-done, f32[512,512]{1,0:T(8,128)S(1)} %copy-done.1), kind=kOutput, calls=%fused_computation.15 | convolution fusion | flops 402784256 | bytes 1835008 | tf_op jit(solution)/shard_map/dot_general | solution.py:36
  180.9 0.7 convolution_bitcast_fusion.1
  181.6 0.3 copy-done.3
  181.8 0.7 fusion.1
  182.6 0.1 copy.7
  182.8 2.3 %collective-permute-done.1 = f32[256,128]{0,1:T(8,128)S(1)} collective-permute-done((f32[256,128]{0,1:T(8,128)S(1)}, f32[256,128]{0,1:T(8,128)S(1)}, u32[]{:S(2)}, u32[]{:S(2)}) %collective-permute-start.1) | collective-permute-done | bytes 131104 | tf_op jit(solution)/shard_map/ppermute | solution.py:12
  185.1 0.1 multiply_reduce_fusion
  185.2 19.6 %psum.31 = f32[128]{0:T(128)S(1)} all-reduce(f32[128]{0:T(128)S(1)} %multiply_reduce_fusion), channel_id=1, replica_groups=mesh['segment'=4,'row'=8] {'row'}, use_global_device_ids=true, to_apply=%region_4.5 | all-reduce | flops 128 | bytes 1024 | tf_op jit(solution)/shard_map/psum | solution.py:48
  204.8 0.5 multiply_sqrt_fusion
  205.3 0.8 copy.8
  (15 shorter events, 0.2 us)
Async XLA Ops:
  7.2 1.0 copy-start
  7.2 3.1 %copy-start.5 = (f32[256,128]{1,0:T(8,128)S(1)}, f32[256,128]{1,0:T(8,128)}, u32[]{:S(2)}) copy-start(f32[256,128]{1,0:T(8,128)} %param.2) | copy-start | bytes 393220
  7.2 91.5 %all-reduce.6.cloned.1.call-start = ((), (), s32[]{:S(2)}) async-start(), calls=%async_computation.1 | async-start | bytes 2621440 | tf_op jit(solution)/shard_map/psum | solution.py:30
  11.9 166.7 %all-reduce.4.cloned.1.call-start = ((), (), s32[]{:S(2)}) async-start(), calls=%async_computation | async-start | bytes 524288 | tf_op jit(solution)/shard_map/psum | solution.py:30
  98.7 1.8 copy-start.1
  100.3 1.0 copy-start.4
  102.9 4.4 %collective-permute-start = (f32[256,128]{0,1:T(8,128)S(1)}, f32[256,128]{0,1:T(8,128)S(1)}, u32[]{:S(2)}, u32[]{:S(2)}) collective-permute-start(f32[256,128]{0,1:T(8,128)S(1)} %fusion.2), channel_id=1, source_target_pairs={{0,8},{8,16},{16,24},{24,0},{1,9},{9,17},{17,25},{25,1},{2,10},{10... | collective-permute-start | bytes 393224 | tf_op jit(solution)/shard_map/ppermute | solution.py:12
  180.9 1.0 copy-start.3
  182.5 2.6 %collective-permute-start.1 = (f32[256,128]{0,1:T(8,128)S(1)}, f32[256,128]{0,1:T(8,128)S(1)}, u32[]{:S(2)}, u32[]{:S(2)}) collective-permute-start(f32[256,128]{0,1:T(8,128)S(1)} %fusion.1), channel_id=1, source_target_pairs={{0,24},{8,0},{16,8},{24,16},{1,25},{9,1},{17,9},{25,17},{2,26},{10... | collective-permute-start | bytes 393224 | tf_op jit(solution)/shard_map/ppermute | solution.py:12
  182.8 23.3 %copy-start.2 = (f32[512,512]{1,0:T(8,128)}, f32[512,512]{1,0:T(8,128)S(1)}, u32[]{:S(2)}) copy-start(f32[512,512]{1,0:T(8,128)S(1)} %constant_dynamic-update-slice_fusion) | copy-start | bytes 3145732
Sparse Core Ops, SparseCore 0:
  12.3 86.3 all-reduce.5
  108.6 70.0 all-reduce.3
where the time goes:
time: 213 us
  waiting for transfers between devices  163 us (77%)
  blocking collectives  19.6 us (9%)
  between operations  14.2 us (7%)
  matrix products  11.6 us (5%)
  local copies, waits for them, and re-layouts  3.2 us (2%)
    psum x2, waiting for transfers between devices, per_device(): lax.psum(jnp.dot(basis.T, visit_vec, precision=high, preferred_element_ty...  157 us
    psum x1, blocking collectives, per_device(): sums = lax.psum(jnp.sum(vec * vec, axis=0), 'row')  19.6 us
    ppermute x2, waiting for transfers between devices, shifted(): return lax.ppermute(value, axis, pairs)  6.69 us
  transfers between devices with their start and end apart: 4, of which 4 were waited for; matrix products, arithmetic and copies ran while one was open for 0% of the time, Pallas kernels for 0%

commit v1 on v0

v1 whole, which is shorter than its diff:
```python
import functools

import jax
import jax.numpy as jnp
from jax import lax
from jax.experimental import pallas as pl
from jax.experimental.pallas import tpu as pltpu
from jax.sharding import PartitionSpec as P

TICKS = 2
MESH = pl.DeviceIdType.MESH
NN = (((1,), (0,)), ((), ()))
NT = (((1,), (1,)), ((), ()))


def split(x):
    high = x.astype(jnp.bfloat16)
    return high, (x - high.astype(jnp.float32)).astype(jnp.bfloat16)


def product(a, high_ref, low_ref, dims):
    rows = a.shape[0]
    high, low = split(a)
    both = lax.dot_general(
        jnp.concatenate([high, low], axis=0), high_ref[...], dims,
        preferred_element_type=jnp.float32,
    )
    rest = lax.dot_general(high, low_ref[...], dims, preferred_element_type=jnp.float32)
    return both[:rows] + (both[rows:] + rest)


def kernel(
    peers, sections, chunks, total_rows,
    v_ref, q_ref, res_ref, coef_ref, rms_ref,
    vt, qh, ql, q2, q2h, q2l, part, inbox, mine, full, csend, cin, ssend, sin,
    rs_send, rs_recv, ag_send, ag_recv, q_sem, c_send, c_recv, s_send, s_recv,
):
    row = lax.axis_index("row")
    seg = lax.axis_index("segment")
    after = lax.rem(seg + 1, sections)
    before = lax.rem(seg + sections - 1, sections)
    batch, sec = part.shape[1:]
    height = batch // chunks
    groups = height // 8
    blocks = peers // groups
    lanes = sec // blocks

    barrier = pltpu.get_barrier_semaphore()
    for k in range(1, peers):
        pl.semaphore_signal(
            barrier, inc=1, device_id={"row": lax.rem(row + k, peers)}, device_id_type=MESH
        )
    for other in (after, before):
        pl.semaphore_signal(barrier, inc=1, device_id={"segment": other}, device_id_type=MESH)

    def place(c, owner):
        top = pl.multiple_of(c * height + (owner // blocks) * 8, 8)
        left = pl.multiple_of(lax.rem(owner, blocks) * lanes, lanes)
        return pl.ds(top, 8), pl.ds(left, lanes)

    def take(p, c, sem):
        span = inbox.at[p, c, pl.ds(1, peers - 1)]
        pltpu.make_async_copy(span, span, sem).wait()

    high, low = split(q_ref[...])
    qh[...] = high
    ql[...] = low
    vt[...] = v_ref[...].T

    q_copy = pltpu.make_async_remote_copy(
        src_ref=q_ref, dst_ref=q2, send_sem=q_sem.at[0], recv_sem=q_sem.at[1],
        device_id={"segment": before}, device_id_type=MESH,
    )

    for p in range(2 * TICKS):
        now = (qh, ql) if p < 2 else (q2h, q2l)
        prior = (qh, ql) if p - 1 < 2 else (q2h, q2l)
        for c in range(chunks):
            span = pl.ds(c * height, height)
            if p > 0:
                take(p - 1, c, ag_recv.at[p - 1, c])
                vec = vt[span, :] - product(full[p - 1, span, :], *prior, NT)
                vt[span, :] = vec
            else:
                vec = vt[span, :]
            part[p, span, :] = product(vec, *now, NN)
            if p == 0 and c == 0:
                pl.semaphore_wait(barrier, peers + 1)
            for k in range(1, peers):
                peer = lax.rem(row + k, peers)
                pltpu.make_async_remote_copy(
                    src_ref=part.at[(p,) + place(c, peer)],
                    dst_ref=inbox.at[p, c, k],
                    send_sem=rs_send.at[p, c], recv_sem=rs_recv.at[p, c],
                    device_id={"row": peer}, device_id_type=MESH,
                ).start()
        if p == 0:
            q_copy.start()
            coef_ref[...] = jnp.zeros_like(coef_ref)
        if p == 2:
            coef_ref[:, pl.ds(pl.multiple_of(seg * batch, batch), batch)] = (
                full[0] + full[1]
            ).T
        for c in range(chunks):
            own = (p,) + place(c, row)
            take(p, c, rs_recv.at[p, c])
            total = part[own]
            for k in range(1, peers):
                total = total + inbox[p, c, k]
            mine[p, c] = total
            full[own] = total
            for k in range(1, peers):
                pltpu.make_async_remote_copy(
                    src_ref=mine.at[p, c], dst_ref=full.at[own],
                    send_sem=ag_send.at[p, c], recv_sem=ag_recv.at[p, c],
                    device_id={"row": lax.rem(row + k, peers)}, device_id_type=MESH,
                ).start()
        if p == 1:
            q_copy.wait()
            high, low = split(q2[...])
            q2h[...] = high
            q2l[...] = low

    moves = []
    for c in range(chunks):
        span = pl.ds(c * height, height)
        take(3, c, ag_recv.at[3, c])
        csend[span, :] = full[2, span, :] + full[3, span, :]
        move = pltpu.make_async_remote_copy(
            src_ref=csend.at[span], dst_ref=cin.at[span],
            send_sem=c_send.at[c], recv_sem=c_recv.at[c],
            device_id={"segment": after}, device_id_type=MESH,
        )
        move.start()
        moves.append(move)
        vt[span, :] = vt[span, :] - product(full[3, span, :], q2h, q2l, NT)
    res = vt[...].T
    sums = jnp.sum(res * res, axis=0, keepdims=True)
    ssend[...] = jnp.broadcast_to(sums, ssend.shape)
    for k in range(1, peers):
        pltpu.make_async_remote_copy(
            src_ref=ssend, dst_ref=sin.at[k], send_sem=s_send, recv_sem=s_recv,
            device_id={"row": lax.rem(row + k, peers)}, device_id_type=MESH,
        ).start()
    res_ref[...] = res
    for p in range(2 * TICKS):
        for c in range(chunks):
            take(p, c, rs_send.at[p, c])
            take(p, c, ag_send.at[p, c])
    for move in moves:
        move.wait()
    coef_ref[:, pl.ds(pl.multiple_of(before * batch, batch), batch)] = cin[...].T
    some = sin.at[pl.ds(1, peers - 1)]
    pltpu.make_async_copy(some, some, s_recv).wait()
    total = ssend[...]
    for k in range(1, peers):
        total = total + sin[k]
    rms_ref[...] = jnp.sqrt(total[:1] / total_rows)
    pltpu.make_async_copy(some, some, s_send).wait()


def per_device(snapshots, basis):
    sections = lax.axis_size("segment")
    peers = lax.axis_size("row")
    rows, batch = snapshots.shape
    sec = basis.shape[1]
    chunks = max(1, min(CHUNKS, batch * sec // (8 * 128 * peers)))
    height = batch // chunks
    lanes = sec // (peers // (height // 8))
    phases = 2 * TICKS
    f32, bf16 = jnp.float32, jnp.bfloat16
    vmem = pl.BlockSpec(memory_space=pltpu.VMEM)
    dma = pltpu.SemaphoreType.DMA
    res, coef, rms = pl.pallas_call(
        functools.partial(kernel, peers, sections, chunks, rows * peers),
        out_shape=(
            jax.ShapeDtypeStruct((rows, batch), f32),
            jax.ShapeDtypeStruct((sec, batch * sections), f32),
            jax.ShapeDtypeStruct((1, batch), f32),
        ),
        in_specs=[vmem, vmem],
        out_specs=(vmem, vmem, vmem),
        scratch_shapes=[
            pltpu.VMEM((batch, rows), f32),
            pltpu.VMEM((rows, sec), bf16),
            pltpu.VMEM((rows, sec), bf16),
            pltpu.VMEM((rows, sec), f32),
            pltpu.VMEM((rows, sec), bf16),
            pltpu.VMEM((rows, sec), bf16),
            pltpu.VMEM((phases, batch, sec), f32),
            pltpu.VMEM((phases, chunks, peers, 8, lanes), f32),
            pltpu.VMEM((phases, chunks, 8, lanes), f32),
            pltpu.VMEM((phases, batch, sec), f32),
            pltpu.VMEM((batch, sec), f32),
            pltpu.VMEM((batch, sec), f32),
            pltpu.VMEM((8, batch), f32),
            pltpu.VMEM((peers, 8, batch), f32),
            dma((phases, chunks)),
            dma((phases, chunks)),
            dma((phases, chunks)),
            dma((phases, chunks)),
            dma((2,)),
            dma((chunks,)),
            dma((chunks,)),
            dma,
            dma,
        ],
        compiler_params=pltpu.CompilerParams(collective_id=0, has_side_effects=True),
    )(snapshots, basis)
    return (res, coef, rms.reshape(batch))


CHUNKS = 4


def solution(mesh):
    placed = (P("row", "segment"), P("row", "segment"))
    return jax.shard_map(
        per_device,
        mesh=mesh,
        in_specs=placed,
        out_specs=(P("row", "segment"), P("segment", None), P("segment")),
        check_vma=False,
    )
```

time: 213 us -> 65.6 us (0.31)
  waiting for transfers between devices: 163 us -> 0 us
  Pallas kernels: 0 us -> 60.5 us
  blocking collectives: 19.6 us -> 0 us
  between operations: 14.2 us -> 0.64 us
  matrix products: 11.6 us -> 0 us
    psum x2 -> x0, waiting for transfers between devices: 157 us -> none  [per_device(): lax.psum(jnp.dot(basis.T, visit_vec, precision=high, preferred_element_ty...]
    pallas_call x0 -> x1, Pallas kernels: none -> 60.5 us  [per_device(): pl.pallas_call(functools.partial(kernel, peers, sections, chunks, rows *...]
    psum x1 -> x0, blocking collectives: 19.6 us -> none  [per_device(): sums = lax.psum(jnp.sum(vec * vec, axis=0), 'row')]
    dot_general x9 -> x0, matrix products: 11.6 us -> none  [the longest x2 3.21 us: per_device(): jnp.dot(gram, first, precision=high, preferred_element_type=jnp.float32)]
    ppermute x2 -> x0, waiting for transfers between devices: 6.69 us -> none  [shifted(): return lax.ppermute(value, axis, pairs)]
    unnamed x14 -> x5, local copies, waits for them, and re-layouts: 2.93 us -> 4.35 us
  transfers between devices with their start and end apart: 4 -> 0, of which waited for: 4 -> 0; matrix products, arithmetic and copies ran while one was open for 0% -> 0% of each run, Pallas kernels for 0% -> 0%
where the time goes in v1:
time: 65.6 us; the launch traced here: 65.5 us
  Pallas kernels  60.5 us (92%)
  local copies, waits for them, and re-layouts  4.35 us (7%)
    pallas_call x1, Pallas kernels, per_device(): pl.pallas_call(functools.partial(kernel, peers, sections, chunks, rows *...  60.5 us
    unnamed x5, local copies, waits for them, and re-layouts  4.35 us

profile of v1, /device:TPU:0, one launch (start us, length us, event | category | flops | bytes accessed | tf_op | source)
XLA Modules:
  0.0 65.5 jit_solution(8004379196492800843)
XLA Ops:
  0.6 60.5 %shard_map.49 = (f32[256,128]{1,0:T(8,128)}, f32[512,512]{1,0:T(8,128)}, f32[1,128]{1,0:T(1,128)}) custom-call(f32[256,128]{1,0:T(8,128)} %v_ref.1, f32[256,512]{1,0:T(8,128)} %q_ref.1), custom_call_target="tpu_custom_call" | custom-call | tf_op jit(solution)/shard_map/pallas_call | solution.py:174
  61.1 1.6 %copy.8 = f32[256,128]{1,0:T(8,128)} copy(f32[256,128]{1,0:T(8,128)} %get-tuple-element.12) | data formatting | bytes 262144
  62.7 0.0 copy-start
  62.7 2.3 %copy.9 = f32[512,512]{1,0:T(8,128)} copy(f32[512,512]{1,0:T(8,128)} %get-tuple-element.13) | data formatting | bytes 2097152
  64.9 0.0 copy-done
  64.9 0.5 copy.10
Async XLA Ops:
  62.7 2.3 %copy-start = (f32[1,128]{1,0:T(1,128)S(1)}, f32[1,128]{1,0:T(1,128)}, u32[]{:S(2)}) copy-start(f32[1,128]{1,0:T(1,128)} %get-tuple-element.8) | copy-start | bytes 1540

commit v2 on v1

--- a/solution.py
+++ b/solution.py
@@ -30,11 +30,16 @@
 
 
 def kernel(
-    peers, sections, chunks, total_rows,
-    v_ref, q_ref, res_ref, coef_ref, rms_ref,
+    peers, sections, chunks,
+    v_hbm, q_hbm, res_ref, here_ref, there_ref, sums_ref,
+    v_ref, q_ref, in_sem,
     vt, qh, ql, q2, q2h, q2l, part, inbox, mine, full, csend, cin, ssend, sin,
     rs_send, rs_recv, ag_send, ag_recv, q_sem, c_send, c_recv, s_send, s_recv,
 ):
+    q_load = pltpu.make_async_copy(q_hbm, q_ref, in_sem.at[0])
+    v_load = pltpu.make_async_copy(v_hbm, v_ref, in_sem.at[1])
+    q_load.start()
+    v_load.start()
     row = lax.axis_index("row")
     seg = lax.axis_index("segment")
     after = lax.rem(seg + 1, sections)
@@ -62,10 +67,12 @@
         span = inbox.at[p, c, pl.ds(1, peers - 1)]
         pltpu.make_async_copy(span, span, sem).wait()
 
+    v_load.wait()
+    vt[...] = v_ref[...].T
+    q_load.wait()
     high, low = split(q_ref[...])
     qh[...] = high
     ql[...] = low
-    vt[...] = v_ref[...].T
 
     q_copy = pltpu.make_async_remote_copy(
         src_ref=q_ref, dst_ref=q2, send_sem=q_sem.at[0], recv_sem=q_sem.at[1],
@@ -96,11 +103,8 @@
                 ).start()
         if p == 0:
             q_copy.start()
-            coef_ref[...] = jnp.zeros_like(coef_ref)
         if p == 2:
-            coef_ref[:, pl.ds(pl.multiple_of(seg * batch, batch), batch)] = (
-                full[0] + full[1]
-            ).T
+            here_ref[...] = (full[0] + full[1]).T
         for c in range(chunks):
             own = (p,) + place(c, row)
             take(p, c, rs_recv.at[p, c])
@@ -149,14 +153,25 @@
             take(p, c, ag_send.at[p, c])
     for move in moves:
         move.wait()
-    coef_ref[:, pl.ds(pl.multiple_of(before * batch, batch), batch)] = cin[...].T
+    there_ref[...] = cin[...].T
     some = sin.at[pl.ds(1, peers - 1)]
     pltpu.make_async_copy(some, some, s_recv).wait()
     total = ssend[...]
     for k in range(1, peers):
         total = total + sin[k]
-    rms_ref[...] = jnp.sqrt(total[:1] / total_rows)
+    sums_ref[...] = total
     pltpu.make_async_copy(some, some, s_send).wait()
+
+
+def finish(sections, total_rows, res_ref, here_ref, there_ref, sums_ref, out_ref, coef_ref, rms_ref):
+    seg = lax.axis_index("segment")
+    batch = here_ref.shape[1]
+    out_ref[...] = res_ref[...]
+    rms_ref[...] = jnp.sqrt(sums_ref[...][:1] / total_rows)
+    coef_ref[...] = jnp.zeros_like(coef_ref)
+    before = lax.rem(seg + sections - 1, sections)
+    coef_ref[:, pl.ds(pl.multiple_of(seg * batch, batch), batch)] = here_ref[...]
+    coef_ref[:, pl.ds(pl.multiple_of(before * batch, batch), batch)] = there_ref[...]
 
 
 def per_device(snapshots, basis):
@@ -171,16 +186,21 @@
     f32, bf16 = jnp.float32, jnp.bfloat16
     vmem = pl.BlockSpec(memory_space=pltpu.VMEM)
     dma = pltpu.SemaphoreType.DMA
-    res, coef, rms = pl.pallas_call(
-        functools.partial(kernel, peers, sections, chunks, rows * peers),
+    anywhere = pl.BlockSpec(memory_space=pl.ANY)
+    parts = pl.pallas_call(
+        functools.partial(kernel, peers, sections, chunks),
         out_shape=(
             jax.ShapeDtypeStruct((rows, batch), f32),
-            jax.ShapeDtypeStruct((sec, batch * sections), f32),
-            jax.ShapeDtypeStruct((1, batch), f32),
+            jax.ShapeDtypeStruct((sec, batch), f32),
+            jax.ShapeDtypeStruct((sec, batch), f32),
+            jax.ShapeDtypeStruct((8, batch), f32),
         ),
-        in_specs=[vmem, vmem],
-        out_specs=(vmem, vmem, vmem),
+        in_specs=[anywhere, anywhere],
+        out_specs=(vmem, vmem, vmem, vmem),
         scratch_shapes=[
+            pltpu.VMEM((rows, batch), f32),
+            pltpu.VMEM((rows, sec), f32),
+            dma((2,)),
             pltpu.VMEM((batch, rows), f32),
             pltpu.VMEM((rows, sec), bf16),
             pltpu.VMEM((rows, sec), bf16),
@@ -207,6 +227,16 @@
         ],
         compiler_params=pltpu.CompilerParams(collective_id=0, has_side_effects=True),
     )(snapshots, basis)
+    res, coef, rms = pl.pallas_call(
+        functools.partial(finish, sections, rows * peers),
+        out_shape=(
+            jax.ShapeDtypeStruct((rows, batch), f32),
+            jax.ShapeDtypeStruct((sec, batch * sections), f32),
+            jax.ShapeDtypeStruct((1, batch), f32),
+        ),
+        in_specs=[vmem] * 4,
+        out_specs=(vmem, vmem, vmem),
+    )(*parts)
     return (res, coef, rms.reshape(batch))
 
 

time: 65.6 us -> 63.2 us (0.963)
  local copies, waits for them, and re-layouts: 4.35 us -> 0 us
  Pallas kernels: 60.5 us -> 62.4 us
    unnamed x5 -> x0, local copies, waits for them, and re-layouts: 4.35 us -> none
    pallas_call x1 -> x2, Pallas kernels: 60.5 us -> 62.4 us  [the longest x1 60.2 us: per_device(): pl.pallas_call(functools.partial(kernel, peers, sections, chunks), out_sh...]
where the time goes in v2:
time: 63.2 us; the launch traced here: 63 us
  Pallas kernels  62.4 us (99%)
  between operations  0.64 us (1%)
    pallas_call x1, Pallas kernels, per_device(): pl.pallas_call(functools.partial(kernel, peers, sections, chunks), out_sh...  60.2 us
    pallas_call x1, Pallas kernels, per_device(): pl.pallas_call(functools.partial(finish, sections, rows * peers), out_sha...  2.21 us

profile of v2, /device:TPU:0, one launch (start us, length us, event | category | flops | bytes accessed | tf_op | source)
XLA Modules:
  0.0 63.0 jit_solution(1881737653690924994)
XLA Ops:
  0.6 60.2 %shard_map.49 = (f32[256,128]{1,0:T(8,128)}, f32[512,128]{1,0:T(8,128)}, f32[512,128]{1,0:T(8,128)}, f32[8,128]{1,0:T(8,128)}) custom-call(f32[256,128]{1,0:T(8,128)} %v_hbm.1, f32[256,512]{1,0:T(8,128)} %q_hbm.1), custom_call_target="tpu_custom_call" | custom-call | tf_op jit(solution)/shard_map/pallas_call | solution.py:190
  60.8 2.2 %shard_map.50 = (f32[256,128]{1,0:T(8,128)}, f32[512,512]{1,0:T(8,128)}, f32[1,128]{1,0:T(1,128)}) custom-call(f32[256,128]{1,0:T(8,128)} %get-tuple-element.10.res_ref, f32[512,128]{1,0:T(8,128)} %get-tuple-element.11.here_ref, f32[512,128]{1,0:T(8,128)} %get-tuple-element.12.there_ref, f32[8,128]{1,0:T(8,128)} %get-tuple-element.13.sums_ref), custom_call_target="tpu_custom_call" | custom-call | tf_op jit(solution)/shard_map/pallas_call | solution.py:230

commit v3 on v2

--- a/solution.py
+++ b/solution.py
@@ -58,6 +58,8 @@
     for other in (after, before):
         pl.semaphore_signal(barrier, inc=1, device_id={"segment": other}, device_id_type=MESH)
 
+    far = sorted(range(1, peers), key=lambda k: min(k, peers - k))
+
     def place(c, owner):
         top = pl.multiple_of(c * height + (owner // blocks) * 8, 8)
         left = pl.multiple_of(lax.rem(owner, blocks) * lanes, lanes)
@@ -93,7 +95,7 @@
             part[p, span, :] = product(vec, *now, NN)
             if p == 0 and c == 0:
                 pl.semaphore_wait(barrier, peers + 1)
-            for k in range(1, peers):
+            for k in far:
                 peer = lax.rem(row + k, peers)
                 pltpu.make_async_remote_copy(
                     src_ref=part.at[(p,) + place(c, peer)],
@@ -113,7 +115,7 @@
                 total = total + inbox[p, c, k]
             mine[p, c] = total
             full[own] = total
-            for k in range(1, peers):
+            for k in far:
                 pltpu.make_async_remote_copy(
                     src_ref=mine.at[p, c], dst_ref=full.at[own],
                     send_sem=ag_send.at[p, c], recv_sem=ag_recv.at[p, c],
@@ -141,7 +143,7 @@
     res = vt[...].T
     sums = jnp.sum(res * res, axis=0, keepdims=True)
     ssend[...] = jnp.broadcast_to(sums, ssend.shape)
-    for k in range(1, peers):
+    for k in far:
         pltpu.make_async_remote_copy(
             src_ref=ssend, dst_ref=sin.at[k], send_sem=s_send, recv_sem=s_recv,
             device_id={"row": lax.rem(row + k, peers)}, device_id_type=MESH,
@@ -190,10 +192,10 @@
     parts = pl.pallas_call(
         functools.partial(kernel, peers, sections, chunks),
         out_shape=(
-            jax.ShapeDtypeStruct((rows, batch), f32),
-            jax.ShapeDtypeStruct((sec, batch), f32),
-            jax.ShapeDtypeStruct((sec, batch), f32),
-            jax.ShapeDtypeStruct((8, batch), f32),
+            pltpu.VMEM((rows, batch), f32),
+            pltpu.VMEM((sec, batch), f32),
+            pltpu.VMEM((sec, batch), f32),
+            pltpu.VMEM((8, batch), f32),
         ),
         in_specs=[anywhere, anywhere],
         out_specs=(vmem, vmem, vmem, vmem),
@@ -236,7 +238,7 @@
         ),
         in_specs=[vmem] * 4,
         out_specs=(vmem, vmem, vmem),
-    )(*parts)
+    )(*[pltpu.with_memory_space_constraint(p, pltpu.VMEM) for p in parts])
     return (res, coef, rms.reshape(batch))
 
 

time: 63.2 us -> 60.5 us (0.957)
  Pallas kernels: 62.4 us -> 59.7 us
    pallas_call x1, Pallas kernels: 60.2 us -> 58.6 us  [per_device(): pl.pallas_call(functools.partial(kernel, peers, sections, chunks), out_sh...]
    pallas_call x1, Pallas kernels: 2.21 us -> 1.11 us  [per_device(): pl.pallas_call(functools.partial(finish, sections, rows * peers), out_sha...]
where the time goes in v3:
time: 60.5 us; the launch traced here: 60.3 us
  Pallas kernels  59.7 us (99%)
  between operations  0.64 us (1%)
    pallas_call x1, Pallas kernels, per_device(): pl.pallas_call(functools.partial(kernel, peers, sections, chunks), out_sh...  58.6 us

profile of v3, /device:TPU:0, one launch (start us, length us, event | category | flops | bytes accessed | tf_op | source)
XLA Modules:
  0.0 60.3 jit_solution(8294864076321584125)
XLA Ops:
  0.6 58.6 %shard_map.49 = (f32[256,128]{1,0:T(8,128)S(1)}, f32[512,128]{1,0:T(8,128)S(1)}, f32[512,128]{1,0:T(8,128)S(1)}, f32[8,128]{1,0:T(8,128)S(1)}) custom-call(f32[256,128]{1,0:T(8,128)} %v_hbm.1, f32[256,512]{1,0:T(8,128)} %q_hbm.1), custom_call_target="tpu_custom_call" | custom-call | tf_op jit(solution)/shard_map/pallas_call | solution.py:192
  59.2 1.1 %shard_map.50 = (f32[256,128]{1,0:T(8,128)}, f32[512,512]{1,0:T(8,128)}, f32[1,128]{1,0:T(1,128)}) custom-call(f32[256,128]{1,0:T(8,128)S(1)} %get-tuple-element.10.res_ref, f32[512,128]{1,0:T(8,128)S(1)} %get-tuple-element.11.here_ref, f32[512,128]{1,0:T(8,128)S(1)} %get-tuple-element.12.there_ref, f32[8,128]{1,0:T(8,128)S(1)} %get-tuple-element.13.sums_ref), custom_call_target="tpu_custom_call" | custom-call | tf_op jit(solution)/shard_map/pallas_call | solution.py:232

commit v4 on v3

--- a/solution.py
+++ b/solution.py
@@ -139,8 +139,7 @@
         )
         move.start()
         moves.append(move)
-        vt[span, :] = vt[span, :] - product(full[3, span, :], q2h, q2l, NT)
-    res = vt[...].T
+    res = (vt[...] - product(full[3], q2h, q2l, NT)).T
     sums = jnp.sum(res * res, axis=0, keepdims=True)
     ssend[...] = jnp.broadcast_to(sums, ssend.shape)
     for k in far:

time: 60.5 us -> 60.5 us (level)
  no operation moved by 1% of the time
where the time goes in v4:
time: 60.5 us; the launch traced here: 60.3 us
  Pallas kernels  59.7 us (99%)
  between operations  0.64 us (1%)
    pallas_call x1, Pallas kernels, per_device(): pl.pallas_call(functools.partial(kernel, peers, sections, chunks), out_sh...  58.6 us

profile of v4, /device:TPU:0, one launch (start us, length us, event | category | flops | bytes accessed | tf_op | source)
XLA Modules:
  0.0 60.3 jit_solution(16155372413328508882)
XLA Ops:
  0.6 58.6 %shard_map.49 = (f32[256,128]{1,0:T(8,128)S(1)}, f32[512,128]{1,0:T(8,128)S(1)}, f32[512,128]{1,0:T(8,128)S(1)}, f32[8,128]{1,0:T(8,128)S(1)}) custom-call(f32[256,128]{1,0:T(8,128)} %v_hbm.1, f32[256,512]{1,0:T(8,128)} %q_hbm.1), custom_call_target="tpu_custom_call" | custom-call | tf_op jit(solution)/shard_map/pallas_call | solution.py:191
  59.2 1.1 %shard_map.50 = (f32[256,128]{1,0:T(8,128)}, f32[512,512]{1,0:T(8,128)}, f32[1,128]{1,0:T(1,128)}) custom-call(f32[256,128]{1,0:T(8,128)S(1)} %get-tuple-element.10.res_ref, f32[512,128]{1,0:T(8,128)S(1)} %get-tuple-element.11.here_ref, f32[512,128]{1,0:T(8,128)S(1)} %get-tuple-element.12.there_ref, f32[8,128]{1,0:T(8,128)S(1)} %get-tuple-element.13.sums_ref), custom_call_target="tpu_custom_call" | custom-call | tf_op jit(solution)/shard_map/pallas_call | solution.py:231
